TPU v7x, 1024 devices: a whole 4x4x32 slice. The times are simulated.
1024 devices in a mesh: gx: 32 (over z_lo, core), gy: 32 (over x, y, z_hi).
Axes of the slice: x: 4, y: 4, z: 32 (z_hi: 2, z_lo: 16; z = z_hi * 16 + z_lo), core: 2. Of those that a mesh axis runs over, the one named last changes fastest.
Arguments:
- adjoint_fields: float32 [6, 256, 1024, 128], P(None, 'gx', 'gy'), may hold values from -6 to 6
- forward_e: bfloat16 [4, 3, 256, 1024, 128], P(None, None, 'gx', 'gy'), may hold values from -6 to 6
- permittivity: float32 [256, 1024, 128], P('gx', 'gy'), may hold values from 1 to 12
- design_mask: int32 [256, 1024, 128], P('gx', 'gy'), may hold values 0 or 1
- band_offsets: int32 [9], replicated, may hold values from -64 to 64, as said below
- filter_taps: float32 [9], replicated, may hold values from 0.05 to 0.5
Outputs:
- filtered: float32 [256, 1024, 128], P('gx', 'gy')
- adjoint_e: float32 [3, 256, 1024, 128], P(None, 'gx', 'gy')
Inputs may be any that keep to these rules, and one draw needn't show every extreme that they name: `band_offsets`: the offsets are distinct; both -64 and 64 occur.
All inputs are finite; a program needn't handle non-finite values. No bound on the sum of `design_mask` on one device may be relied on, other than what follows from the above.
Results may differ from a plain program's by a relative error of at most 0.0003.
Values sent between devices are 32-bit elements; how exact they have to be, the bound alone decides.
A program may use at most 32 MiB of HBM per device.

v0:
```python
import jax
import jax.numpy as jnp
from jax import lax
from jax.sharding import PartitionSpec as P

ITERS = 4


courant = 0.5


def shifted(value, axis, steps):
    count = lax.axis_size(axis)
    initial, last = (max(0, -steps), min(count, count - steps))
    return lax.ppermute(value, axis, [(source, source + steps) for source in range(initial, last)])


def blank_plane(quantity, along):
    return jnp.zeros_like(lax.index_in_dim(quantity, 0, along, keepdims=False))


def forward_diff(quantity, along, border):
    remainder = lax.slice_in_dim(quantity, 1, quantity.shape[along], axis=along)
    joined = jnp.concatenate([remainder, jnp.expand_dims(border, along)], along)
    return joined - quantity


def backward_diff(quantity, along, border):
    remainder = lax.slice_in_dim(quantity, 0, quantity.shape[along] - 1, axis=along)
    joined = jnp.concatenate([jnp.expand_dims(border, along), remainder], along)
    return quantity - joined


def update_magnetic(electric, magnetic, after_x, after_y):
    elec_x, elec_y, elec_z = electric
    magn_x, magn_y, magn_z = magnetic
    magn_x = magn_x - courant * (
        forward_diff(elec_z, 1, after_y[1]) - forward_diff(elec_y, 2, blank_plane(elec_y, 2))
    )
    magn_y = magn_y - courant * (
        forward_diff(elec_x, 2, blank_plane(elec_x, 2)) - forward_diff(elec_z, 0, after_x[1])
    )
    magn_z = magn_z - courant * (
        forward_diff(elec_y, 0, after_x[0]) - forward_diff(elec_x, 1, after_y[0])
    )
    return (magn_x, magn_y, magn_z)


def update_electric(electric, magnetic, factor, before_x, before_y):
    elec_x, elec_y, elec_z = electric
    magn_x, magn_y, magn_z = magnetic
    elec_x = elec_x + factor * (
        backward_diff(magn_z, 1, before_y[1]) - backward_diff(magn_y, 2, blank_plane(magn_y, 2))
    )
    elec_y = elec_y + factor * (
        backward_diff(magn_x, 2, blank_plane(magn_x, 2)) - backward_diff(magn_z, 0, before_x[1])
    )
    elec_z = elec_z + factor * (
        backward_diff(magn_y, 0, before_x[0]) - backward_diff(magn_x, 1, before_y[0])
    )
    return (elec_x, elec_y, elec_z)


def intersection(stored, electric):
    stored = stored.astype(jnp.float32)
    return stored[0] * electric[0] + stored[1] * electric[1] + stored[2] * electric[2]


def from_x_side(planes, shift_by):
    return shifted(planes, "gx", shift_by)


def from_y_side(planes, shift_by):
    return shifted(planes, "gy", shift_by)


def apply_band(pencil, band_offsets, filter_taps):
    total = pencil.shape[0]
    reach = total // 4
    padded = jnp.pad(pencil, ((reach, reach), (0, 0)))
    result = jnp.zeros(pencil.shape, jnp.float32)
    for index in range(band_offsets.shape[0]):
        start = reach + band_offsets[index]
        result = result + filter_taps[index] * lax.dynamic_slice_in_dim(padded, start, total, 0)
    return result


def shards(adjoint_fields, forward_e, permittivity, design_mask, band_offsets, filter_taps):
    width_x, width_y, width_z = permittivity.shape
    gradient = jnp.zeros(permittivity.shape, jnp.float32)
    electric = (adjoint_fields[0], adjoint_fields[1], adjoint_fields[2])
    magnetic = (adjoint_fields[3], adjoint_fields[4], adjoint_fields[5])
    factor = courant / permittivity
    for turn in range(ITERS):
        after_x = from_x_side(jnp.stack([electric[1][0], electric[2][0]]), -1)
        after_y = from_y_side(jnp.stack([electric[0][:, 0], electric[2][:, 0]]), -1)
        magnetic = update_magnetic(
            electric, magnetic, (after_x[0], after_x[1]), (after_y[0], after_y[1])
        )
        before_x = from_x_side(jnp.stack([magnetic[1][-1], magnetic[2][-1]]), 1)
        before_y = from_y_side(jnp.stack([magnetic[0][:, -1], magnetic[2][:, -1]]), 1)
        electric = update_electric(
            electric, magnetic, factor, (before_x[0], before_x[1]), (before_y[0], before_y[1])
        )
        gradient = gradient + intersection(forward_e[turn], electric)
    final_e = jnp.stack(list(electric))
    masked = gradient * design_mask.astype(jnp.float32)
    columns = masked.reshape(width_x, width_y * width_z)
    lines = apply_band(
        lax.all_to_all(columns, "gx", split_axis=1, concat_axis=0, tiled=True),
        band_offsets,
        filter_taps,
    )
    returned = lax.all_to_all(lines, "gx", split_axis=0, concat_axis=1, tiled=True)
    filtered = returned.reshape(width_x, width_y, width_z)
    return (filtered, final_e)


def solution(mesh):
    return jax.shard_map(
        shards,
        mesh=mesh,
        in_specs=(
            P(None, "gx", "gy", None),
            P(None, None, "gx", "gy", None),
            P("gx", "gy", None),
            P("gx", "gy", None),
            P(),
            P(),
        ),
        out_specs=(P("gx", "gy", None), P(None, "gx", "gy", None)),
        check_vma=False,
    )
```

profile of v0, /device:TPU:7, one launch (start us, length us, event | category | flops | bytes accessed | tf_op | source)
XLA Modules:
  0.0 299.3 jit_solution(1619910846878543246)
XLA Ops:
  0.6 1.3 fusion.118
  1.9 0.0 copy-start.1
  1.9 0.2 copy_bitcast_fusion.3
  2.1 31.5 %collective-permute-start.1 = (f32[2,8,128]{2,1,0:T(8,128)S(1)}, f32[2,8,128]{2,1,0:T(8,128)S(1)}, u32[]{:S(2)}, u32[]{:S(2)}) collective-permute-start(f32[2,8,128]{2,1,0:T(8,128)S(1)} %pad_maximum_fusion.9), channel_id=1, source_target_pairs={{1,0},{2,1},{3,2},{4,3},{5,4},{6,5},{7,6},{8,7},{9,8},{10,9},{11,1... | collective-permute-start | bytes 24584 | tf_op jit(solution)/shard_map/ppermute | solution.py:15
  33.7 0.7 fusion.120
  34.4 2.9 collective-permute-start
  37.3 1.0 fusion.119
  38.3 0.1 fusion.117
  38.4 0.1 copy_convert_fusion.2
  38.5 0.1 copy_convert_fusion
  38.6 0.1 copy_bitcast_fusion
  38.8 0.1 slice.653
  38.9 0.1 copy.127
  39.0 0.1 slice.648
  39.1 0.5 collective-permute-done
  39.7 0.6 fusion.47
  40.4 14.9 %collective-permute-start.2 = (f32[2,8,128]{2,1,0:T(8,128)S(1)}, f32[2,8,128]{2,1,0:T(8,128)S(1)}, u32[]{:S(2)}, u32[]{:S(2)}) collective-permute-start(f32[2,8,128]{2,1,0:T(8,128)S(1)} %pad_maximum_fusion.10), channel_id=1, source_target_pairs={{0,1},{1,2},{2,3},{3,4},{4,5},{5,6},{6,7},{7,8},{8,9},{9,10},{10,1... | collective-permute-start | bytes 24584 | tf_op jit(solution)/shard_map/ppermute | solution.py:15
  55.4 0.0 copy-start
  55.4 4.8 %collective-permute-start.3 = (f32[2,32,128]{2,0,1:T(2,128)S(1)}, f32[2,32,128]{2,0,1:T(2,128)S(1)}, u32[]{:S(2)}, u32[]{:S(2)}) collective-permute-start(f32[2,32,128]{2,0,1:T(2,128)S(1)} %pad_maximum_fusion.2), channel_id=1, source_target_pairs={{0,32},{32,64},{64,96},{96,128},{128,160},{160,192},{192,224},{224... | collective-permute-start | bytes 98312 | tf_op jit(solution)/shard_map/ppermute | solution.py:15
  60.2 6.0 %collective-permute-done.2 = f32[2,8,128]{2,1,0:T(8,128)S(1)} collective-permute-done((f32[2,8,128]{2,1,0:T(8,128)S(1)}, f32[2,8,128]{2,1,0:T(8,128)S(1)}, u32[]{:S(2)}, u32[]{:S(2)}) %collective-permute-start.2) | collective-permute-done | bytes 8224 | tf_op jit(solution)/shard_map/ppermute | solution.py:15
  66.2 0.4 fusion.50
  66.7 16.7 %collective-permute-start.5 = (f32[2,8,128]{2,1,0:T(8,128)S(1)}, f32[2,8,128]{2,1,0:T(8,128)S(1)}, u32[]{:S(2)}, u32[]{:S(2)}) collective-permute-start(f32[2,8,128]{2,1,0:T(8,128)S(1)} %pad_maximum_fusion.11), channel_id=1, source_target_pairs={{1,0},{2,1},{3,2},{4,3},{5,4},{6,5},{7,6},{8,7},{9,8},{10,9},{11,1... | collective-permute-start | bytes 24584 | tf_op jit(solution)/shard_map/ppermute | solution.py:15
  83.5 0.1 slice.678
  83.6 0.1 slice.683
  83.7 5.2 %collective-permute-start.4 = (f32[2,32,128]{2,0,1:T(2,128)S(1)}, f32[2,32,128]{2,0,1:T(2,128)S(1)}, u32[]{:S(2)}, u32[]{:S(2)}) collective-permute-start(f32[2,32,128]{2,0,1:T(2,128)S(1)} %pad_maximum_fusion.3), channel_id=1, source_target_pairs={{32,0},{64,32},{96,64},{128,96},{160,128},{192,160},{224,192},{256... | collective-permute-start | bytes 98312 | tf_op jit(solution)/shard_map/ppermute | solution.py:15
  88.9 0.6 collective-permute-done.5
  89.5 1.7 collective-permute-done.4
  91.1 0.2 fusion.65
  91.4 11.1 %collective-permute-start.6 = (f32[2,8,128]{2,1,0:T(8,128)S(1)}, f32[2,8,128]{2,1,0:T(8,128)S(1)}, u32[]{:S(2)}, u32[]{:S(2)}) collective-permute-start(f32[2,8,128]{2,1,0:T(8,128)S(1)} %pad_maximum_fusion.12), channel_id=1, source_target_pairs={{0,1},{1,2},{2,3},{3,4},{4,5},{5,6},{6,7},{7,8},{8,9},{9,10},{10,1... | collective-permute-start | bytes 24584 | tf_op jit(solution)/shard_map/ppermute | solution.py:15
  102.6 6.9 %collective-permute-start.7 = (f32[2,32,128]{2,0,1:T(2,128)S(1)}, f32[2,32,128]{2,0,1:T(2,128)S(1)}, u32[]{:S(2)}, u32[]{:S(2)}) collective-permute-start(f32[2,32,128]{2,0,1:T(2,128)S(1)} %pad_maximum_fusion.4), channel_id=1, source_target_pairs={{0,32},{32,64},{64,96},{96,128},{128,160},{160,192},{192,224},{224... | collective-permute-start | bytes 98312 | tf_op jit(solution)/shard_map/ppermute | solution.py:15
  109.5 7.9 %collective-permute-done.6 = f32[2,8,128]{2,1,0:T(8,128)S(1)} collective-permute-done((f32[2,8,128]{2,1,0:T(8,128)S(1)}, f32[2,8,128]{2,1,0:T(8,128)S(1)}, u32[]{:S(2)}, u32[]{:S(2)}) %collective-permute-start.6) | collective-permute-done | bytes 8224 | tf_op jit(solution)/shard_map/ppermute | solution.py:15
  117.4 0.2 fusion.68
  117.7 14.8 %collective-permute-start.9 = (f32[2,8,128]{2,1,0:T(8,128)S(1)}, f32[2,8,128]{2,1,0:T(8,128)S(1)}, u32[]{:S(2)}, u32[]{:S(2)}) collective-permute-start(f32[2,8,128]{2,1,0:T(8,128)S(1)} %pad_maximum_fusion.13), channel_id=1, source_target_pairs={{1,0},{2,1},{3,2},{4,3},{5,4},{6,5},{7,6},{8,7},{9,8},{10,9},{11,1... | collective-permute-start | bytes 24584 | tf_op jit(solution)/shard_map/ppermute | solution.py:15
  132.6 0.1 slice.709
  132.7 0.1 slice.714
  132.9 7.4 %collective-permute-start.8 = (f32[2,32,128]{2,0,1:T(2,128)S(1)}, f32[2,32,128]{2,0,1:T(2,128)S(1)}, u32[]{:S(2)}, u32[]{:S(2)}) collective-permute-start(f32[2,32,128]{2,0,1:T(2,128)S(1)} %pad_maximum_fusion.5), channel_id=1, source_target_pairs={{32,0},{64,32},{96,64},{128,96},{160,128},{192,160},{224,192},{256... | collective-permute-start | bytes 98312 | tf_op jit(solution)/shard_map/ppermute | solution.py:15
  140.3 0.2 collective-permute-done.9
  140.4 2.1 collective-permute-done.8
  142.5 0.2 fusion.83
  142.8 6.7 %collective-permute-start.10 = (f32[2,8,128]{2,1,0:T(8,128)S(1)}, f32[2,8,128]{2,1,0:T(8,128)S(1)}, u32[]{:S(2)}, u32[]{:S(2)}) collective-permute-start(f32[2,8,128]{2,1,0:T(8,128)S(1)} %pad_maximum_fusion.14), channel_id=1, source_target_pairs={{0,1},{1,2},{2,3},{3,4},{4,5},{5,6},{6,7},{7,8},{8,9},{9,10},{10,1... | collective-permute-start | bytes 24584 | tf_op jit(solution)/shard_map/ppermute | solution.py:15
  149.6 9.2 %collective-permute-start.11 = (f32[2,32,128]{2,0,1:T(2,128)S(1)}, f32[2,32,128]{2,0,1:T(2,128)S(1)}, u32[]{:S(2)}, u32[]{:S(2)}) collective-permute-start(f32[2,32,128]{2,0,1:T(2,128)S(1)} %pad_maximum_fusion.6), channel_id=1, source_target_pairs={{0,32},{32,64},{64,96},{96,128},{128,160},{160,192},{192,224},{224... | collective-permute-start | bytes 98312 | tf_op jit(solution)/shard_map/ppermute | solution.py:15
  158.8 10.0 %collective-permute-done.10 = f32[2,8,128]{2,1,0:T(8,128)S(1)} collective-permute-done((f32[2,8,128]{2,1,0:T(8,128)S(1)}, f32[2,8,128]{2,1,0:T(8,128)S(1)}, u32[]{:S(2)}, u32[]{:S(2)}) %collective-permute-start.10) | collective-permute-done | bytes 8224 | tf_op jit(solution)/shard_map/ppermute | solution.py:15
  168.9 0.2 fusion.86
  169.2 12.6 %collective-permute-start.13 = (f32[2,8,128]{2,1,0:T(8,128)S(1)}, f32[2,8,128]{2,1,0:T(8,128)S(1)}, u32[]{:S(2)}, u32[]{:S(2)}) collective-permute-start(f32[2,8,128]{2,1,0:T(8,128)S(1)} %pad_maximum_fusion.15), channel_id=1, source_target_pairs={{1,0},{2,1},{3,2},{4,3},{5,4},{6,5},{7,6},{8,7},{9,8},{10,9},{11,1... | collective-permute-start | bytes 24584 | tf_op jit(solution)/shard_map/ppermute | solution.py:15
  181.8 0.1 slice.740
  181.9 0.1 slice.745
  182.1 9.6 %collective-permute-start.12 = (f32[2,32,128]{2,0,1:T(2,128)S(1)}, f32[2,32,128]{2,0,1:T(2,128)S(1)}, u32[]{:S(2)}, u32[]{:S(2)}) collective-permute-start(f32[2,32,128]{2,0,1:T(2,128)S(1)} %pad_maximum_fusion.7), channel_id=1, source_target_pairs={{32,0},{64,32},{96,64},{128,96},{160,128},{192,160},{224,192},{256... | collective-permute-start | bytes 98312 | tf_op jit(solution)/shard_map/ppermute | solution.py:15
  191.7 0.2 collective-permute-done.13
  191.9 2.0 collective-permute-done.12
  193.9 0.2 fusion.101
  194.2 5.0 %collective-permute-start.14 = (f32[2,8,128]{2,1,0:T(8,128)S(1)}, f32[2,8,128]{2,1,0:T(8,128)S(1)}, u32[]{:S(2)}, u32[]{:S(2)}) collective-permute-start(f32[2,8,128]{2,1,0:T(8,128)S(1)} %pad_maximum_fusion.16), channel_id=1, source_target_pairs={{0,1},{1,2},{2,3},{3,4},{4,5},{5,6},{6,7},{7,8},{8,9},{9,10},{10,1... | collective-permute-start | bytes 24584 | tf_op jit(solution)/shard_map/ppermute | solution.py:15
  199.3 0.0 copy-start.2
  199.3 8.9 %collective-permute-start.15 = (f32[2,32,128]{2,0,1:T(2,128)S(1)}, f32[2,32,128]{2,0,1:T(2,128)S(1)}, u32[]{:S(2)}, u32[]{:S(2)}) collective-permute-start(f32[2,32,128]{2,0,1:T(2,128)S(1)} %pad_maximum_fusion.8), channel_id=1, source_target_pairs={{0,32},{32,64},{64,96},{96,128},{128,160},{160,192},{192,224},{224... | collective-permute-start | bytes 98312 | tf_op jit(solution)/shard_map/ppermute | solution.py:15
  208.2 11.7 %collective-permute-done.14 = f32[2,8,128]{2,1,0:T(8,128)S(1)} collective-permute-done((f32[2,8,128]{2,1,0:T(8,128)S(1)}, f32[2,8,128]{2,1,0:T(8,128)S(1)}, u32[]{:S(2)}, u32[]{:S(2)}) %collective-permute-start.14) | collective-permute-done | bytes 8224 | tf_op jit(solution)/shard_map/ppermute | solution.py:15
  220.0 1.2 fusion.21
  221.1 15.0 %all-to-all-start = ((f32[8,32,128]{2,0,1:T(8,128)}), f32[8,32,128]{2,0,1:T(8,128)S(1)}, u32[]{:S(2)}, u32[]{:S(2)}) async-start(f32[8,32,128]{2,0,1:T(8,128)} %get-tuple-element.4), calls=%async_computation | async-start | bytes 262144 | tf_op jit(solution)/shard_map/all_to_all | solution.py:110
  236.2 0.7 fusion.130
  248.3 0.7 fusion.129
  249.0 10.3 %all-to-all-done = f32[8,32,128]{2,0,1:T(8,128)S(1)} async-done(((f32[8,32,128]{2,0,1:T(8,128)}), f32[8,32,128]{2,0,1:T(8,128)S(1)}, u32[]{:S(2)}, u32[]{:S(2)}) %all-to-all-start) | async-done | bytes 131104 | tf_op jit(solution)/shard_map/all_to_all | solution.py:110
  259.4 6.6 %fusion.9 = f32[32,8,128]{2,1,0:T(8,128)} fusion(s32[]{:T(128)S(6)} %select_n.27, f32[256,128]{1,0:T(8,128)S(1)} %bitcast.272, s32[]{:T(128)S(6)} %select_n.28, s32[]{:T(128)S(6)} %select_n.29, s32[]{:T(128)S(6)} %select_n.30, s32[]{:T(128)S(6)} %select_n.31, s32[]{:T(128)S(6)} %select_n.32, s32[]{:T(128)S(6)} %select_n.33, s32[]{:T(128)S(6)} %select_n.34, ...), kind=kLoop, calls=%fused_computation.23 | loop fusion | flops 557056 | bytes 262216 | tf_op jit(solution)/shard_map/all_to_all | solution.py:114
  266.0 9.4 %all-to-all-start.1 = ((f32[32,8,128]{2,1,0:T(8,128)}), f32[32,8,128]{2,1,0:T(8,128)S(1)}, u32[]{:S(2)}, u32[]{:S(2)}) async-start(f32[32,8,128]{2,1,0:T(8,128)} %fusion.9), calls=%async_computation.1 | async-start | bytes 262144 | tf_op jit(solution)/shard_map/all_to_all | solution.py:114
  275.5 0.8 copy.47
  276.3 22.4 %all-to-all-done.1 = f32[32,8,128]{2,1,0:T(8,128)S(1)} async-done(((f32[32,8,128]{2,1,0:T(8,128)}), f32[32,8,128]{2,1,0:T(8,128)S(1)}, u32[]{:S(2)}, u32[]{:S(2)}) %all-to-all-start.1) | async-done | bytes 131104 | tf_op jit(solution)/shard_map/all_to_all | solution.py:114
  298.6 0.7 copy.46
  (97 shorter events, 1.1 us)
Async XLA Ops:
  1.9 36.4 %copy-start.1 = (bf16[4,3,8,32,128]{4,3,2,1,0:T(8,128)(2,1)S(1)}, bf16[4,3,8,32,128]{4,3,2,1,0:T(8,128)(2,1)}, u32[]{:S(2)}) copy-start(bf16[4,3,8,32,128]{4,3,2,1,0:T(8,128)(2,1)} %param.7) | copy-start | bytes 2359300
  2.1 37.0 %collective-permute-start.1 = (f32[2,8,128]{2,1,0:T(8,128)S(1)}, f32[2,8,128]{2,1,0:T(8,128)S(1)}, u32[]{:S(2)}, u32[]{:S(2)}) collective-permute-start(f32[2,8,128]{2,1,0:T(8,128)S(1)} %pad_maximum_fusion.9), channel_id=1, source_target_pairs={{1,0},{2,1},{3,2},{4,3},{5,4},{6,5},{7,6},{8,7},{9,8},{10,9},{11,1... | collective-permute-start | bytes 24584 | tf_op jit(solution)/shard_map/ppermute | solution.py:15
  34.4 5.2 %collective-permute-start = (f32[2,32,128]{2,0,1:T(2,128)S(1)}, f32[2,32,128]{2,0,1:T(2,128)S(1)}, u32[]{:S(2)}, u32[]{:S(2)}) collective-permute-start(f32[2,32,128]{2,0,1:T(2,128)S(1)} %pad_maximum_fusion.1), channel_id=1, source_target_pairs={{32,0},{64,32},{96,64},{128,96},{160,128},{192,160},{224,192},{256... | collective-permute-start | bytes 98312 | tf_op jit(solution)/shard_map/ppermute | solution.py:15
  40.4 25.8 %collective-permute-start.2 = (f32[2,8,128]{2,1,0:T(8,128)S(1)}, f32[2,8,128]{2,1,0:T(8,128)S(1)}, u32[]{:S(2)}, u32[]{:S(2)}) collective-permute-start(f32[2,8,128]{2,1,0:T(8,128)S(1)} %pad_maximum_fusion.10), channel_id=1, source_target_pairs={{0,1},{1,2},{2,3},{3,4},{4,5},{5,6},{6,7},{7,8},{8,9},{9,10},{10,1... | collective-permute-start | bytes 24584 | tf_op jit(solution)/shard_map/ppermute | solution.py:15
  55.4 10.9 %copy-start = (f32[8,32,128]{2,1,0:T(8,128)S(1)}, f32[8,32,128]{2,1,0:T(8,128)}, u32[]{:S(2)}) copy-start(f32[8,32,128]{2,1,0:T(8,128)} %param.8) | copy-start | bytes 393220
  55.4 10.8 %collective-permute-start.3 = (f32[2,32,128]{2,0,1:T(2,128)S(1)}, f32[2,32,128]{2,0,1:T(2,128)S(1)}, u32[]{:S(2)}, u32[]{:S(2)}) collective-permute-start(f32[2,32,128]{2,0,1:T(2,128)S(1)} %pad_maximum_fusion.2), channel_id=1, source_target_pairs={{0,32},{32,64},{64,96},{96,128},{128,160},{160,192},{192,224},{224... | collective-permute-start | bytes 98312 | tf_op jit(solution)/shard_map/ppermute | solution.py:15
  66.7 22.7 %collective-permute-start.5 = (f32[2,8,128]{2,1,0:T(8,128)S(1)}, f32[2,8,128]{2,1,0:T(8,128)S(1)}, u32[]{:S(2)}, u32[]{:S(2)}) collective-permute-start(f32[2,8,128]{2,1,0:T(8,128)S(1)} %pad_maximum_fusion.11), channel_id=1, source_target_pairs={{1,0},{2,1},{3,2},{4,3},{5,4},{6,5},{7,6},{8,7},{9,8},{10,9},{11,1... | collective-permute-start | bytes 24584 | tf_op jit(solution)/shard_map/ppermute | solution.py:15
  83.7 7.4 %collective-permute-start.4 = (f32[2,32,128]{2,0,1:T(2,128)S(1)}, f32[2,32,128]{2,0,1:T(2,128)S(1)}, u32[]{:S(2)}, u32[]{:S(2)}) collective-permute-start(f32[2,32,128]{2,0,1:T(2,128)S(1)} %pad_maximum_fusion.3), channel_id=1, source_target_pairs={{32,0},{64,32},{96,64},{128,96},{160,128},{192,160},{224,192},{256... | collective-permute-start | bytes 98312 | tf_op jit(solution)/shard_map/ppermute | solution.py:15
  91.4 26.0 %collective-permute-start.6 = (f32[2,8,128]{2,1,0:T(8,128)S(1)}, f32[2,8,128]{2,1,0:T(8,128)S(1)}, u32[]{:S(2)}, u32[]{:S(2)}) collective-permute-start(f32[2,8,128]{2,1,0:T(8,128)S(1)} %pad_maximum_fusion.12), channel_id=1, source_target_pairs={{0,1},{1,2},{2,3},{3,4},{4,5},{5,6},{6,7},{7,8},{8,9},{9,10},{10,1... | collective-permute-start | bytes 24584 | tf_op jit(solution)/shard_map/ppermute | solution.py:15
  102.6 14.8 %collective-permute-start.7 = (f32[2,32,128]{2,0,1:T(2,128)S(1)}, f32[2,32,128]{2,0,1:T(2,128)S(1)}, u32[]{:S(2)}, u32[]{:S(2)}) collective-permute-start(f32[2,32,128]{2,0,1:T(2,128)S(1)} %pad_maximum_fusion.4), channel_id=1, source_target_pairs={{0,32},{32,64},{64,96},{96,128},{128,160},{160,192},{192,224},{224... | collective-permute-start | bytes 98312 | tf_op jit(solution)/shard_map/ppermute | solution.py:15
  117.7 22.7 %collective-permute-start.9 = (f32[2,8,128]{2,1,0:T(8,128)S(1)}, f32[2,8,128]{2,1,0:T(8,128)S(1)}, u32[]{:S(2)}, u32[]{:S(2)}) collective-permute-start(f32[2,8,128]{2,1,0:T(8,128)S(1)} %pad_maximum_fusion.13), channel_id=1, source_target_pairs={{1,0},{2,1},{3,2},{4,3},{5,4},{6,5},{7,6},{8,7},{9,8},{10,9},{11,1... | collective-permute-start | bytes 24584 | tf_op jit(solution)/shard_map/ppermute | solution.py:15
  132.9 9.6 %collective-permute-start.8 = (f32[2,32,128]{2,0,1:T(2,128)S(1)}, f32[2,32,128]{2,0,1:T(2,128)S(1)}, u32[]{:S(2)}, u32[]{:S(2)}) collective-permute-start(f32[2,32,128]{2,0,1:T(2,128)S(1)} %pad_maximum_fusion.5), channel_id=1, source_target_pairs={{32,0},{64,32},{96,64},{128,96},{160,128},{192,160},{224,192},{256... | collective-permute-start | bytes 98312 | tf_op jit(solution)/shard_map/ppermute | solution.py:15
  142.8 26.1 %collective-permute-start.10 = (f32[2,8,128]{2,1,0:T(8,128)S(1)}, f32[2,8,128]{2,1,0:T(8,128)S(1)}, u32[]{:S(2)}, u32[]{:S(2)}) collective-permute-start(f32[2,8,128]{2,1,0:T(8,128)S(1)} %pad_maximum_fusion.14), channel_id=1, source_target_pairs={{0,1},{1,2},{2,3},{3,4},{4,5},{5,6},{6,7},{7,8},{8,9},{9,10},{10,1... | collective-permute-start | bytes 24584 | tf_op jit(solution)/shard_map/ppermute | solution.py:15
  149.6 19.2 %collective-permute-start.11 = (f32[2,32,128]{2,0,1:T(2,128)S(1)}, f32[2,32,128]{2,0,1:T(2,128)S(1)}, u32[]{:S(2)}, u32[]{:S(2)}) collective-permute-start(f32[2,32,128]{2,0,1:T(2,128)S(1)} %pad_maximum_fusion.6), channel_id=1, source_target_pairs={{0,32},{32,64},{64,96},{96,128},{128,160},{160,192},{192,224},{224... | collective-permute-start | bytes 98312 | tf_op jit(solution)/shard_map/ppermute | solution.py:15
  169.2 22.7 %collective-permute-start.13 = (f32[2,8,128]{2,1,0:T(8,128)S(1)}, f32[2,8,128]{2,1,0:T(8,128)S(1)}, u32[]{:S(2)}, u32[]{:S(2)}) collective-permute-start(f32[2,8,128]{2,1,0:T(8,128)S(1)} %pad_maximum_fusion.15), channel_id=1, source_target_pairs={{1,0},{2,1},{3,2},{4,3},{5,4},{6,5},{7,6},{8,7},{9,8},{10,9},{11,1... | collective-permute-start | bytes 24584 | tf_op jit(solution)/shard_map/ppermute | solution.py:15
  182.1 11.8 %collective-permute-start.12 = (f32[2,32,128]{2,0,1:T(2,128)S(1)}, f32[2,32,128]{2,0,1:T(2,128)S(1)}, u32[]{:S(2)}, u32[]{:S(2)}) collective-permute-start(f32[2,32,128]{2,0,1:T(2,128)S(1)} %pad_maximum_fusion.7), channel_id=1, source_target_pairs={{32,0},{64,32},{96,64},{128,96},{160,128},{192,160},{224,192},{256... | collective-permute-start | bytes 98312 | tf_op jit(solution)/shard_map/ppermute | solution.py:15
  194.2 25.7 %collective-permute-start.14 = (f32[2,8,128]{2,1,0:T(8,128)S(1)}, f32[2,8,128]{2,1,0:T(8,128)S(1)}, u32[]{:S(2)}, u32[]{:S(2)}) collective-permute-start(f32[2,8,128]{2,1,0:T(8,128)S(1)} %pad_maximum_fusion.16), channel_id=1, source_target_pairs={{0,1},{1,2},{2,3},{3,4},{4,5},{5,6},{6,7},{7,8},{8,9},{9,10},{10,1... | collective-permute-start | bytes 24584 | tf_op jit(solution)/shard_map/ppermute | solution.py:15
  199.3 20.7 %copy-start.2 = (s32[8,32,128]{2,1,0:T(8,128)S(1)}, s32[8,32,128]{2,1,0:T(8,128)}, u32[]{:S(2)}) copy-start(s32[8,32,128]{2,1,0:T(8,128)} %param.9) | copy-start | bytes 393220
  199.3 20.6 %collective-permute-start.15 = (f32[2,32,128]{2,0,1:T(2,128)S(1)}, f32[2,32,128]{2,0,1:T(2,128)S(1)}, u32[]{:S(2)}, u32[]{:S(2)}) collective-permute-start(f32[2,32,128]{2,0,1:T(2,128)S(1)} %pad_maximum_fusion.8), channel_id=1, source_target_pairs={{0,32},{32,64},{64,96},{96,128},{128,160},{160,192},{192,224},{224... | collective-permute-start | bytes 98312 | tf_op jit(solution)/shard_map/ppermute | solution.py:15
  220.0 16.2 %copy-start.3 = (s32[9]{0:T(128)S(1)}, s32[9]{0:T(128)}, u32[]{:S(2)}) copy-start(s32[9]{0:T(128)} %param.10) | copy-start | bytes 112
  221.1 27.2 %copy-start.4 = (f32[9]{0:T(128)S(1)}, f32[9]{0:T(128)}, u32[]{:S(2)}) copy-start(f32[9]{0:T(128)} %param.11) | copy-start | bytes 112
  221.1 38.2 %all-to-all-start = ((f32[8,32,128]{2,0,1:T(8,128)}), f32[8,32,128]{2,0,1:T(8,128)S(1)}, u32[]{:S(2)}, u32[]{:S(2)}) async-start(f32[8,32,128]{2,0,1:T(8,128)} %get-tuple-element.4), calls=%async_computation | async-start | bytes 262144 | tf_op jit(solution)/shard_map/all_to_all | solution.py:110
  266.0 32.6 %all-to-all-start.1 = ((f32[32,8,128]{2,1,0:T(8,128)}), f32[32,8,128]{2,1,0:T(8,128)S(1)}, u32[]{:S(2)}, u32[]{:S(2)}) async-start(f32[32,8,128]{2,1,0:T(8,128)} %fusion.9), calls=%async_computation.1 | async-start | bytes 262144 | tf_op jit(solution)/shard_map/all_to_all | solution.py:114
where the time goes:
time: 301 us; the launch traced here: 299 us
  starting transfers between devices  193 us (64%)
  waiting for transfers between devices  75.5 us (25%)
  between operations  13 us (4%)
  other arithmetic  10.4 us (3%)
  local copies, waits for them, and re-layouts  7.76 us (3%)
    ppermute x16, starting transfers between devices, shifted(): lax.ppermute(value, axis, [(source, source + steps) for source in range(i...  168 us
    ppermute x16, waiting for transfers between devices, shifted(): lax.ppermute(value, axis, [(source, source + steps) for source in range(i...  42.8 us
    all_to_all x1, waiting for transfers between devices, shards(): lax.all_to_all(lines, 'gx', split_axis=0, concat_axis=1, tiled=True)  22.4 us
    all_to_all x1, starting transfers between devices, shards(): lax.all_to_all(columns, 'gx', split_axis=1, concat_axis=0, tiled=True)  15 us
    all_to_all x1, waiting for transfers between devices, shards(): lax.all_to_all(columns, 'gx', split_axis=1, concat_axis=0, tiled=True)  10.3 us
    all_to_all x1, starting transfers between devices, shards(): lax.all_to_all(lines, 'gx', split_axis=0, concat_axis=1, tiled=True)  9.41 us
    all_to_all x1, other arithmetic, shards(): lax.all_to_all(lines, 'gx', split_axis=0, concat_axis=1, tiled=True)  6.62 us
  transfers between devices with their start and end apart: 18, of which 13 were waited for; matrix products, arithmetic and copies ran while one was open for 2% of the time, Pallas kernels for 0%

commit v1 on v0

v1 whole, which is shorter than its diff:
```python
import functools

import jax
import jax.numpy as jnp
from jax import lax
from jax.experimental import pallas as pl
from jax.experimental.pallas import tpu as pltpu
from jax.sharding import PartitionSpec as P

ITERS = 4
BAND = 9
REACH = 64
courant = 0.5

MESH = pl.DeviceIdType.MESH
F32 = jnp.float32
ROWS = 8
EDGE = 4
WIDE = ROWS + 2 * EDGE
NY = 32
NZ = 128
LEFT_BOUND = (0, 2, 3, 4, 5)
RIGHT_BOUND = (1, 6, 7, 8, 9)
MESSAGES = 10
CHIPS = 4


def kernel(
    nx, ny,
    fields_hbm, stored_hbm, perm_hbm, mask_hbm, off_ref, tap_ref,
    filt_ref, final_ref,
    F, FE, PV, MV, G, SB, RB, D, CS, GS, WA, WB,
    load_sem, x_send, x_recv, far_send, far_recv, fwd_send, fwd_recv,
    za_send, za_recv, pa_send, pa_recv, zb_send, zb_recv, pb_send, pb_recv,
):
    gx, gy = lax.axis_index("gx"), lax.axis_index("gy")
    core, chip, chips = gx % 2, gx // 2, nx // 2
    has_left, has_right = gx > 0, gx < nx - 1
    has_below, has_above = gy > 0, gy < ny - 1

    loads = [
        pltpu.make_async_copy(fields_hbm, F.at[pl.ds(0, 6), pl.ds(EDGE, ROWS)], load_sem.at[0]),
        pltpu.make_async_copy(perm_hbm, PV, load_sem.at[1]),
        pltpu.make_async_copy(stored_hbm, FE, load_sem.at[2]),
        pltpu.make_async_copy(mask_hbm, MV, load_sem.at[3]),
    ]
    for load in loads:
        load.start()

    def clear(ref, length):
        @pl.loop(0, length)
        def _(i):
            ref[i] = jnp.zeros(ref.shape[1:], F32)

    RB[...] = jnp.zeros(RB.shape, F32)

    @pl.when(jnp.logical_not(has_left))
    def _():
        for k in range(7):
            for r in range(EDGE):
                F[k, r] = jnp.zeros((NY, NZ), F32)

    @pl.when(jnp.logical_not(has_right))
    def _():
        for k in range(7):
            for r in range(EDGE):
                F[k, EDGE + ROWS + r] = jnp.zeros((NY, NZ), F32)

    @pl.when((gx < ROWS) | (gx >= nx - ROWS))
    def _():
        clear(WA, 17 * ROWS)
        clear(WB, 17 * ROWS)

    barrier = pltpu.get_barrier_semaphore()

    def greet(condition, where):
        @pl.when(condition)
        def _():
            pl.semaphore_signal(barrier, inc=1, device_id=where, device_id_type=MESH)

    up_chip, down_chip = chip < chips - 1, chip > 0
    greet(has_below, {"gy": gy - 1})
    greet(has_above, {"gy": gy + 1})
    greet(has_left, {"gx": gx - 1})
    greet(has_right, {"gx": gx + 1})
    greet(down_chip, {"gx": gx - 2})
    greet(up_chip, {"gx": gx + 2})

    iy = lax.broadcasted_iota(jnp.int32, (NY, NZ), 0)
    iz = lax.broadcasted_iota(jnp.int32, (NY, NZ), 1)
    sub = lax.broadcasted_iota(jnp.int32, (8, NZ), 0)
    lane = lax.broadcasted_iota(jnp.int32, (8, NZ), 1)

    loads[0].wait()
    loads[1].wait()

    @pl.loop(0, ROWS)
    def _(r):
        c = courant / PV[r]
        F[6, EDGE + r] = c
        row = pl.ds(r + 8, 1)
        SB[0, 0, row] = c[0:1]
        SB[0, 1, row] = c[1:2]
        SB[1, 0, row] = c[31:32]
        SB[1, 1, row] = c[30:31]

    def level0(x):
        row = pl.ds(x + 4, 1)
        SB[2, 0, row] = F[0, x, pl.ds(0, 1), :]
        SB[2, 1, row] = F[2, x, pl.ds(0, 1), :]

    @pl.loop(EDGE, EDGE + ROWS)
    def _(x):
        level0(x)

    def count(condition):
        return jnp.where(condition, 1, 0)

    pl.semaphore_wait(
        barrier,
        count(has_below) + count(has_above) + count(has_left) + count(has_right) + count(down_chip) + count(up_chip),
    )

    def to_left():
        return pltpu.make_async_remote_copy(
            src_ref=F.at[:, pl.ds(EDGE, EDGE)], dst_ref=F.at[:, pl.ds(EDGE + ROWS, EDGE)],
            send_sem=x_send.at[0], recv_sem=x_recv.at[0], device_id={"gx": gx - 1}, device_id_type=MESH,
        )

    def to_right():
        return pltpu.make_async_remote_copy(
            src_ref=F.at[:, pl.ds(ROWS, EDGE)], dst_ref=F.at[:, pl.ds(0, EDGE)],
            send_sem=x_send.at[1], recv_sem=x_recv.at[1], device_id={"gx": gx + 1}, device_id_type=MESH,
        )

    pl.when(has_left)(lambda: to_left().start())
    pl.when(has_right)(lambda: to_right().start())

    middle = pl.ds(8, 8)

    def far(m):
        where = {"gy": gy - 1} if m in LEFT_BOUND else {"gy": gy + 1}
        return pltpu.make_async_remote_copy(
            src_ref=SB.at[m, :, middle], dst_ref=RB.at[m, :, middle],
            send_sem=far_send.at[m], recv_sem=far_recv.at[m], device_id=where, device_id_type=MESH,
        )

    def sends(m):
        return has_below if m in LEFT_BOUND else has_above

    def receives(m):
        return has_above if m in LEFT_BOUND else has_below

    def post(m):
        pl.when(sends(m))(lambda: far(m).start())

    post(0)
    post(1)
    post(2)

    pl.when(has_right)(lambda: to_left().wait_recv())
    pl.when(has_left)(lambda: to_right().wait_recv())
    pl.when(has_left)(lambda: to_left().wait_send())
    pl.when(has_right)(lambda: to_right().wait_send())

    for x in (*range(0, EDGE), *range(EDGE + ROWS, WIDE)):
        level0(x)
    loads[2].wait()
    loads[3].wait()

    def half(x):
        outside = (jnp.logical_not(has_left) & (x < EDGE)) | (jnp.logical_not(has_right) & (x >= EDGE + ROWS))
        return jnp.where(outside, 0.0, courant).astype(F32)

    def next_y(v):
        return jnp.where(iy < NY - 1, pltpu.roll(v, NY - 1, 0), 0.0)

    def last_y(v):
        return jnp.where(iy > 0, pltpu.roll(v, 1, 0), 0.0)

    def next_z(v):
        return jnp.where(iz < NZ - 1, pltpu.roll(v, NZ - 1, 1), 0.0)

    def last_z(v):
        return jnp.where(iz > 0, pltpu.roll(v, 1, 1), 0.0)

    def magnetic(x, step):
        s = half(x)
        ex, ey, ez = F[0, x], F[1, x], F[2, x]
        hx = F[3, x] - s * ((next_y(ez) - ez) - (next_z(ey) - ey))
        hy = F[4, x] - s * ((next_z(ex) - ex) - (F[2, x + 1] - ez))
        hz = F[5, x] - s * ((F[1, x + 1] - ey) - (next_y(ex) - ex))
        F[3, x], F[4, x], F[5, x] = hx, hy, hz
        row = pl.ds(x + 4, 1)
        SB[6 + step, 0, row] = hx[NY - 1 : NY]
        SB[6 + step, 1, row] = hz[NY - 1 : NY]
        return ex, ey, ez, hx, hy, hz

    def both(x, step, graded):
        ex, ey, ez, hx, hy, hz = magnetic(x, step)
        c = F[6, x]
        ex = ex + c * ((hz - last_y(hz)) - (hy - last_z(hy)))
        ey = ey + c * ((hx - last_z(hx)) - (hz - F[5, x - 1]))
        ez = ez + c * ((hy - F[4, x - 1]) - (hx - last_y(hx)))
        F[0, x], F[1, x], F[2, x] = ex, ey, ez
        if step < ITERS - 1:
            row = pl.ds(x + 4, 1)
            SB[3 + step, 0, row] = ex[0:1]
            SB[3 + step, 1, row] = ez[0:1]
        if graded:
            r = x - EDGE
            g = FE[step, 0, r].astype(F32) * ex + FE[step, 1, r].astype(F32) * ey + FE[step, 2, r].astype(F32) * ez
            G[r] = g if step == 0 else G[r] + g

    for step in range(ITERS):
        magnetic(step, step)
        lax.fori_loop(step + 1, EDGE, lambda x, _: (both(x, step, False), 0)[1], 0)
        lax.fori_loop(EDGE, EDGE + ROWS, lambda x, _: (both(x, step, True), 0)[1], 0)
        lax.fori_loop(EDGE + ROWS, WIDE - 1 - step, lambda x, _: (both(x, step, False), 0)[1], 0)
        post(6 + step)
        if step < ITERS - 1:
            post(3 + step)

    lower = sub < 4

    def gather(W, z_send, z_recv, p_send, p_recv):
        def slot(s):
            return W.at[pl.ds(ROWS * s, ROWS)]

        def relay(way, k):
            sign = -1 if way == 0 else 1
            return pltpu.make_async_remote_copy(
                src_ref=slot(8 + sign * 2 * (k - 1)), dst_ref=slot(8 + sign * 2 * k),
                send_sem=z_send.at[way, k - 1], recv_sem=z_recv.at[way, k - 1],
                device_id={"gx": gx - 2 * sign}, device_id_type=MESH,
            )

        def exists(way, k):
            return chip >= k if way == 0 else chip + k <= chips - 1

        def relays(way, k):
            onward = up_chip if way == 0 else down_chip
            return onward if k == 1 else onward & exists(way, k - 1)

        def across(way, k):
            sign = -1 if way == 0 else 1
            s = 8 + sign * 2 * k
            i = s // 2 - 1 + core
            return pltpu.make_async_remote_copy(
                src_ref=slot(s), dst_ref=slot(2 * i + 1),
                send_sem=p_send.at[s // 2], recv_sem=p_recv.at[i],
                device_id={"gx": gx + 1 - 2 * core}, device_id_type=MESH,
            )

        def crosses(way, k):
            if k == 0:
                return None
            known = exists(way, k)
            if k == CHIPS:
                known = known & (core == 1 if way == 0 else core == 0)
            return known

        def begin():
            pl.when(relays(0, 1))(lambda: relay(0, 1).start())
            pl.when(relays(1, 1))(lambda: relay(1, 1).start())
            across(0, 0).start()

        def step(k):
            for way in (0, 1):
                pl.when(exists(way, k))(functools.partial(lambda w: relay(w, k).wait_recv(), way))
                if k < CHIPS:
                    pl.when(relays(way, k + 1))(functools.partial(lambda w: relay(w, k + 1).start(), way))
                pl.when(crosses(way, k))(functools.partial(lambda w: across(w, k).start(), way))

        def finish():
            for i in range(8):
                other = gx + 2 * i + 1 - 8
                copy = pltpu.make_async_remote_copy(
                    src_ref=slot(2 * i + 1), dst_ref=slot(2 * i + 1),
                    send_sem=p_send.at[0], recv_sem=p_recv.at[i],
                    device_id={"gx": gx + 1 - 2 * core}, device_id_type=MESH,
                )
                pl.when((other >= 0) & (other < nx))(copy.wait_recv)

        def drain():
            across(0, 0).wait_send()
            for k in range(1, CHIPS + 1):
                for way in (0, 1):
                    pl.when(relays(way, k))(functools.partial(lambda w, j: relay(w, j).wait_send(), way, k))
                    pl.when(crosses(way, k))(functools.partial(lambda w, j: across(w, j).wait_send(), way, k))

        return begin, step, finish, drain

    begin_a, step_a, finish_a, drain_a = gather(WA, za_send, za_recv, pa_send, pa_recv)
    begin_b, step_b, finish_b, drain_b = gather(WB, zb_send, zb_recv, pb_send, pb_recv)

    @pl.loop(0, ROWS)
    def _(r):
        m = G[r] * MV[r].astype(F32)
        WA[8 * ROWS + r, pl.ds(0, 16), :] = m[8:24]
        WA[8 * ROWS + r, pl.ds(16, 8), :] = jnp.where(lower, m[24:32], m[0:8])

    begin_a()
    for k in range(1, CHIPS + 1):
        step_a(k)

    def forward(m, way):
        tile = 2 if way == 0 else 0
        where = {"gx": gx - 1} if way == 0 else {"gx": gx + 1}
        return pltpu.make_async_remote_copy(
            src_ref=RB.at[m, :, middle], dst_ref=RB.at[m, :, pl.ds(8 * tile, 8)],
            send_sem=fwd_send.at[m, way], recv_sem=fwd_recv.at[m, way], device_id=where, device_id_type=MESH,
        )

    order = (0, 1, 2, 6, 3, 7, 4, 8, 5, 9)
    for m in order:
        pl.when(receives(m))(functools.partial(lambda i: far(i).wait_recv(), m))
        pl.when(receives(m) & has_left)(functools.partial(lambda i: forward(i, 0).start(), m))
        pl.when(receives(m) & has_right)(functools.partial(lambda i: forward(i, 1).start(), m))

    for k in range(6):
        for side in range(2):
            D[side, k] = jnp.zeros((WIDE, 8, NZ), F32)

    def arrived(m):
        pl.when(receives(m) & has_right)(functools.partial(lambda i: forward(i, 0).wait_recv(), m))
        pl.when(receives(m) & has_left)(functools.partial(lambda i: forward(i, 1).wait_recv(), m))

    for m in order:
        arrived(m)

    @pl.loop(0, WIDE)
    def _(x):
        row = pl.ds(x + 4, 1)
        c = F[6, x]
        near, next_near = RB[1, 0, row], RB[1, 1, row]
        CS[0, x] = jnp.where(lower, c[0:8], jnp.where(sub == 7, near, jnp.where(sub == 6, next_near, 0.0)))
        near, next_near = RB[0, 0, row], RB[0, 1, row]
        CS[1, x] = jnp.where(lower, jnp.where(sub == 0, near, jnp.where(sub == 1, next_near, 0.0)), c[24:32])

    inflow = jnp.where(has_below, 1.0, 0.0).astype(F32)

    def next_s(v, trace):
        return pltpu.roll(v, 7, 0) + jnp.where(sub == 7, trace, 0.0)

    def last_s(v, trace):
        return pltpu.roll(v, 1, 0) + jnp.where(sub == 0, trace, 0.0)

    def up(v):
        return jnp.where(lane < NZ - 1, pltpu.roll(v, NZ - 1, 1), 0.0)

    def down(v):
        return jnp.where(lane > 0, pltpu.roll(v, 1, 1), 0.0)

    def strip_magnetic(side, x, step):
        s = half(x)
        row = pl.ds(x + 4, 1)
        if side == 0:
            tx, tz = SB[2 + step, 0, row] * inflow, SB[2 + step, 1, row] * inflow
        else:
            tx, tz = RB[2 + step, 0, row], RB[2 + step, 1, row]
        ex, ey, ez = D[side, 0, x], D[side, 1, x], D[side, 2, x]
        hx = D[side, 3, x] - s * ((next_s(ez, tz) - ez) - (up(ey) - ey))
        hy = D[side, 4, x] - s * ((up(ex) - ex) - (D[side, 2, x + 1] - ez))
        hz = D[side, 5, x] - s * ((D[side, 1, x + 1] - ey) - (next_s(ex, tx) - ex))
        D[side, 3, x], D[side, 4, x], D[side, 5, x] = hx, hy, hz
        return ex, ey, ez, hx, hy, hz

    def strip_both(side, x, step, graded):
        ex, ey, ez, hx, hy, hz = strip_magnetic(side, x, step)
        row = pl.ds(x + 4, 1)
        planes = RB if side == 0 else SB
        tx, tz = planes[6 + step, 0, row], planes[6 + step, 1, row]
        c = CS[side, x]
        ex = ex + c * ((hz - last_s(hz, tz)) - (hy - down(hy)))
        ey = ey + c * ((hx - down(hx)) - (hz - D[side, 5, x - 1]))
        ez = ez + c * ((hy - D[side, 4, x - 1]) - (hx - last_s(hx, tx)))
        D[side, 0, x], D[side, 1, x], D[side, 2, x] = ex, ey, ez
        if graded:
            r = x - EDGE
            if side == 0:
                stored = [FE[step, k, r, pl.ds(0, 16), :].astype(F32)[0:8] for k in range(3)]
            else:
                stored = [FE[step, k, r, pl.ds(16, 16), :].astype(F32)[8:16] for k in range(3)]
            g = stored[0] * ex + stored[1] * ey + stored[2] * ez
            GS[side, r] = g if step == 0 else GS[side, r] + g

    def strips(x, step, graded):
        strip_both(0, x, step, graded)
        strip_both(1, x, step, graded)
        return 0

    for step in range(ITERS):
        strip_magnetic(0, step, step)
        strip_magnetic(1, step, step)
        lax.fori_loop(step + 1, EDGE, lambda x, _: strips(x, step, False), 0)
        lax.fori_loop(EDGE, EDGE + ROWS, lambda x, _: strips(x, step, True), 0)
        lax.fori_loop(EDGE + ROWS, WIDE - 1 - step, lambda x, _: strips(x, step, False), 0)

    @pl.loop(0, ROWS)
    def _(r):
        g = jnp.where(lower, G[r, pl.ds(0, 8), :] + GS[0, r], G[r, pl.ds(24, 8), :] + GS[1, r])
        mask = jnp.where(lower, MV[r, pl.ds(0, 8), :], MV[r, pl.ds(24, 8), :])
        WB[8 * ROWS + r] = g * mask.astype(F32)

    begin_b()

    @pl.loop(0, ROWS)
    def _(r):
        x = r + EDGE
        for k in range(3):
            e = F[k, x]
            final_ref[k, r, pl.ds(8, 16), :] = e[8:24]
            final_ref[k, r, pl.ds(0, 8), :] = e[0:8] + jnp.where(lower, D[0, k, x], 0.0)
            final_ref[k, r, pl.ds(24, 8), :] = e[24:32] + jnp.where(lower, 0.0, D[1, k, x])

    finish_a()
    for k in range(1, CHIPS + 1):
        step_b(k)
    finish_b()

    taps = [tap_ref[b] for b in range(BAND)]
    starts = [off_ref[b] + REACH for b in range(BAND)]

    @pl.loop(0, ROWS)
    def _(r):
        wide, thin = taps[0] * WA[starts[0] + r], taps[0] * WB[starts[0] + r]
        for b in range(1, BAND):
            wide = wide + taps[b] * WA[starts[b] + r]
            thin = thin + taps[b] * WB[starts[b] + r]
        mixed = wide[16:24]
        filt_ref[r, pl.ds(8, 16), :] = wide[0:16]
        filt_ref[r, pl.ds(0, 8), :] = jnp.where(lower, thin, mixed)
        filt_ref[r, pl.ds(24, 8), :] = jnp.where(lower, mixed, thin)

    for m in range(MESSAGES):
        pl.when(sends(m))(functools.partial(lambda i: far(i).wait_send(), m))
        pl.when(receives(m) & has_left)(functools.partial(lambda i: forward(i, 0).wait_send(), m))
        pl.when(receives(m) & has_right)(functools.partial(lambda i: forward(i, 1).wait_send(), m))
    drain_a()
    drain_b()


def solution(mesh):
    nx, ny = mesh.shape["gx"], mesh.shape["gy"]

    def shards(adjoint_fields, forward_e, permittivity, design_mask, band_offsets, filter_taps):
        dma = pltpu.SemaphoreType.DMA
        hbm, vmem, smem = (pl.BlockSpec(memory_space=s) for s in (pl.ANY, pltpu.VMEM, pltpu.SMEM))
        return pl.pallas_call(
            functools.partial(kernel, nx, ny),
            out_shape=(
                jax.ShapeDtypeStruct((ROWS, NY, NZ), F32),
                jax.ShapeDtypeStruct((3, ROWS, NY, NZ), F32),
            ),
            in_specs=[hbm, hbm, hbm, hbm, smem, smem],
            out_specs=(vmem, vmem),
            scratch_shapes=[
                pltpu.VMEM((7, WIDE, NY, NZ), F32),
                pltpu.VMEM((ITERS, 3, ROWS, NY, NZ), jnp.bfloat16),
                pltpu.VMEM((ROWS, NY, NZ), F32),
                pltpu.VMEM((ROWS, NY, NZ), jnp.int32),
                pltpu.VMEM((ROWS, NY, NZ), F32),
                pltpu.VMEM((MESSAGES, 2, 24, NZ), F32),
                pltpu.VMEM((MESSAGES, 2, 24, NZ), F32),
                pltpu.VMEM((2, 6, WIDE, 8, NZ), F32),
                pltpu.VMEM((2, WIDE, 8, NZ), F32),
                pltpu.VMEM((2, ROWS, 8, NZ), F32),
                pltpu.VMEM((17 * ROWS, 24, NZ), F32),
                pltpu.VMEM((17 * ROWS, 8, NZ), F32),
                dma((4,)), dma((2,)), dma((2,)),
                dma((MESSAGES,)), dma((MESSAGES,)), dma((MESSAGES, 2)), dma((MESSAGES, 2)),
                dma((2, CHIPS)), dma((2, CHIPS)), dma((9,)), dma((8,)),
                dma((2, CHIPS)), dma((2, CHIPS)), dma((9,)), dma((8,)),
            ],
            compiler_params=pltpu.CompilerParams(collective_id=0, has_side_effects=True),
            name="adjoint_yee_filter",
        )(adjoint_fields, forward_e, permittivity, design_mask, band_offsets, filter_taps)

    return jax.shard_map(
        shards,
        mesh=mesh,
        in_specs=(
            P(None, "gx", "gy", None),
            P(None, None, "gx", "gy", None),
            P("gx", "gy", None),
            P("gx", "gy", None),
            P(),
            P(),
        ),
        out_specs=(P("gx", "gy", None), P(None, "gx", "gy", None)),
        check_vma=False,
    )
```

time: 301 us -> 101 us (0.34)
  starting transfers between devices: 193 us -> 0 us
  Pallas kernels: 0 us -> 96.1 us
  waiting for transfers between devices: 75.5 us -> 0 us
  between operations: 13 us -> 0.64 us
  other arithmetic: 10.4 us -> 0 us
  local copies, waits for them, and re-layouts: 7.76 us -> 3.33 us
    ppermute x16 -> x0, starting transfers between devices: 168 us -> none  [shifted(): lax.ppermute(value, axis, [(source, source + steps) for source in range(i...]
    pallas_call x0 -> x1, Pallas kernels: none -> 96.1 us  [shards(): pl.pallas_call(functools.partial(kernel, nx, ny), out_shape=(jax.ShapeDty...]
    ppermute x16 -> x0, waiting for transfers between devices: 42.8 us -> none  [shifted(): lax.ppermute(value, axis, [(source, source + steps) for source in range(i...]
    all_to_all x2 -> x0, waiting for transfers between devices: 32.7 us -> none  [the longest x1 22.4 us: shards(): lax.all_to_all(lines, 'gx', split_axis=0, concat_axis=1, tiled=True)]
    all_to_all x2 -> x0, starting transfers between devices: 24.4 us -> none  [the longest x1 15 us: shards(): lax.all_to_all(columns, 'gx', split_axis=1, concat_axis=0, tiled=True)]
    all_to_all x1 -> x0, other arithmetic: 6.62 us -> none  [shards(): lax.all_to_all(lines, 'gx', split_axis=0, concat_axis=1, tiled=True)]
    slice x59 -> x0, local copies, waits for them, and re-layouts: 5.94 us -> none  [the longest x24 2.03 us: forward_diff(): remainder = lax.slice_in_dim(quantity, 1, quantity.shape[along], axis=along)]
  transfers between devices with their start and end apart: 18 -> 0, of which waited for: 13 -> 0; matrix products, arithmetic and copies ran while one was open for 2% -> 0% of each run, Pallas kernels for 0% -> 0%
where the time goes in v1:
time: 101 us; the launch traced here: 100 us
  Pallas kernels  96.1 us (95%)
  local copies, waits for them, and re-layouts  3.33 us (3%)
    pallas_call x1, Pallas kernels, shards(): pl.pallas_call(functools.partial(kernel, nx, ny), out_shape=(jax.ShapeDty...  96.1 us
    unnamed x2, local copies, waits for them, and re-layouts  3.33 us

profile of v1, /device:TPU:7, one launch (start us, length us, event | category | flops | bytes accessed | tf_op | source)
XLA Modules:
  0.0 100.0 jit_solution(11198602649444299716)
XLA Ops:
  0.6 96.1 %adjoint_yee_filter.1 = (f32[8,32,128]{2,1,0:T(8,128)}, f32[3,8,32,128]{3,2,1,0:T(8,128)}) custom-call(f32[6,8,32,128]{3,2,1,0:T(8,128)} %fields_hbm.1, bf16[4,3,8,32,128]{4,3,2,1,0:T(8,128)(2,1)} %stored_hbm.1, f32[8,32,128]{2,1,0:T(8,128)} %perm_hbm.1, s32[8,32,128]{2,1,0:T(8,128)} %mask_hbm.1, s32[9]{0:T(128)} %off_ref.1, f32[9]{0:T(128)} %tap_ref.1), custom_call_target="tpu_custom_call" | custom-call | tf_op jit(solution)/shard_map/adjoint_yee_filter/pallas_call | solution.py:450
  96.7 1.6 %copy.10 = f32[8,32,128]{2,1,0:T(8,128)} copy(f32[8,32,128]{2,1,0:T(8,128)} %get-tuple-element.4) | data formatting | bytes 262144
  98.3 1.8 %copy.11 = f32[3,8,32,128]{3,2,1,0:T(8,128)} copy(f32[3,8,32,128]{3,2,1,0:T(8,128)} %get-tuple-element.5) | data formatting | bytes 786432

commit v2 on v1

--- a/solution.py
+++ b/solution.py
@@ -29,7 +29,7 @@
     nx, ny,
     fields_hbm, stored_hbm, perm_hbm, mask_hbm, off_ref, tap_ref,
     filt_ref, final_ref,
-    F, FE, PV, MV, G, SB, RB, D, CS, GS, WA, WB,
+    F, FE, PV, MV, G, SB, RB, T, D, CS, GS, WA, WB,
     load_sem, x_send, x_recv, far_send, far_recv, fwd_send, fwd_recv,
     za_send, za_recv, pa_send, pa_recv, zb_send, zb_recv, pb_send, pb_recv,
 ):
@@ -78,13 +78,17 @@
         def _():
             pl.semaphore_signal(barrier, inc=1, device_id=where, device_id_type=MESH)
 
-    up_chip, down_chip = chip < chips - 1, chip > 0
+    def chip_at(way, k):
+        return chip >= k if way == 0 else chip + k <= chips - 1
+
+    up_chip, down_chip = chip_at(1, 1), chip_at(0, 1)
     greet(has_below, {"gy": gy - 1})
     greet(has_above, {"gy": gy + 1})
     greet(has_left, {"gx": gx - 1})
     greet(has_right, {"gx": gx + 1})
-    greet(down_chip, {"gx": gx - 2})
-    greet(up_chip, {"gx": gx + 2})
+    for k in range(1, CHIPS + 1):
+        greet(chip_at(0, k), {"gx": gx - 2 * k})
+        greet(chip_at(1, k), {"gx": gx + 2 * k})
 
     iy = lax.broadcasted_iota(jnp.int32, (NY, NZ), 0)
     iz = lax.broadcasted_iota(jnp.int32, (NY, NZ), 1)
@@ -118,23 +122,31 @@
 
     pl.semaphore_wait(
         barrier,
-        count(has_below) + count(has_above) + count(has_left) + count(has_right) + count(down_chip) + count(up_chip),
+        count(has_below) + count(has_above) + count(has_left) + count(has_right)
+        + jnp.minimum(chip, CHIPS) + jnp.minimum(chips - 1 - chip, CHIPS),
     )
 
-    def to_left():
+    pieces = (pl.ds(0, 8), pl.ds(NY - 8, 8), pl.ds(8, NY - 16))
+
+    def border(way, piece):
+        here, there = (EDGE, EDGE + ROWS) if way == 0 else (ROWS, 0)
         return pltpu.make_async_remote_copy(
-            src_ref=F.at[:, pl.ds(EDGE, EDGE)], dst_ref=F.at[:, pl.ds(EDGE + ROWS, EDGE)],
-            send_sem=x_send.at[0], recv_sem=x_recv.at[0], device_id={"gx": gx - 1}, device_id_type=MESH,
-        )
-
-    def to_right():
-        return pltpu.make_async_remote_copy(
-            src_ref=F.at[:, pl.ds(ROWS, EDGE)], dst_ref=F.at[:, pl.ds(0, EDGE)],
-            send_sem=x_send.at[1], recv_sem=x_recv.at[1], device_id={"gx": gx + 1}, device_id_type=MESH,
-        )
-
-    pl.when(has_left)(lambda: to_left().start())
-    pl.when(has_right)(lambda: to_right().start())
+            src_ref=F.at[:, pl.ds(here, EDGE), pieces[piece]], dst_ref=F.at[:, pl.ds(there, EDGE), pieces[piece]],
+            send_sem=x_send.at[way, piece], recv_sem=x_recv.at[way, piece],
+            device_id={"gx": gx - 1} if way == 0 else {"gx": gx + 1}, device_id_type=MESH,
+        )
+
+    def each_border(which, act):
+        for piece in which:
+            pl.when(has_left)(functools.partial(lambda p: act(border(0, p), 0), piece))
+            pl.when(has_right)(functools.partial(lambda p: act(border(1, p), 1), piece))
+
+    def border_arrives(which):
+        for piece in which:
+            pl.when(has_right)(functools.partial(lambda p: border(0, p).wait_recv(), piece))
+            pl.when(has_left)(functools.partial(lambda p: border(1, p).wait_recv(), piece))
+
+    each_border((0, 1), lambda copy, _: copy.start())
 
     middle = pl.ds(8, 8)
 
@@ -158,20 +170,75 @@
     post(1)
     post(2)
 
-    pl.when(has_right)(lambda: to_left().wait_recv())
-    pl.when(has_left)(lambda: to_right().wait_recv())
-    pl.when(has_left)(lambda: to_left().wait_send())
-    pl.when(has_right)(lambda: to_right().wait_send())
+    each_border((2,), lambda copy, _: copy.start())
+    border_arrives((0, 1))
 
     for x in (*range(0, EDGE), *range(EDGE + ROWS, WIDE)):
         level0(x)
-    loads[2].wait()
-    loads[3].wait()
-
     def half(x):
         outside = (jnp.logical_not(has_left) & (x < EDGE)) | (jnp.logical_not(has_right) & (x >= EDGE + ROWS))
         return jnp.where(outside, 0.0, courant).astype(F32)
 
+    def up(v):
+        return jnp.where(lane < NZ - 1, pltpu.roll(v, NZ - 1, 1), 0.0)
+
+    def down(v):
+        return jnp.where(lane > 0, pltpu.roll(v, 1, 1), 0.0)
+
+    def step_strips(step, old, new, c_of, e_ahead, h_behind):
+        for x in range(step, WIDE - 1 - step):
+            s = half(x)
+            for side in range(2):
+                ex, ey, ez = (old(side, k, x) for k in range(3))
+                ahead = e_ahead(side, x)
+                new[side, 3, x] = old(side, 3, x) - s * ((ahead(ez, 1) - ez) - (up(ey) - ey))
+                new[side, 4, x] = old(side, 4, x) - s * ((up(ex) - ex) - (old(side, 2, x + 1) - ez))
+                new[side, 5, x] = old(side, 5, x) - s * ((old(side, 1, x + 1) - ey) - (ahead(ex, 0) - ex))
+        for x in range(step + 1, WIDE - 1 - step):
+            for side in range(2):
+                hx, hy, hz = (new[side, k, x] for k in range(3, 6))
+                behind = h_behind(side, x)
+                c = c_of(side, x)
+                new[side, 0, x] = old(side, 0, x) + c * ((hz - behind(hz, 1)) - (hy - down(hy)))
+                new[side, 1, x] = old(side, 1, x) + c * ((hx - down(hx)) - (hz - new[side, 5, x - 1]))
+                new[side, 2, x] = old(side, 2, x) + c * ((hy - new[side, 4, x - 1]) - (hx - behind(hx, 0)))
+
+    tile = (pl.ds(0, 8), pl.ds(NY - 8, 8))
+
+    def from_block(side, k, x):
+        return F[k, x, tile[side], :]
+
+    def from_strip(side, k, x):
+        return T[side, k, x]
+
+    def closed_ahead(side, x):
+        return lambda v, _: jnp.where(sub < 7, pltpu.roll(v, 7, 0), 0.0)
+
+    def closed_behind(side, x):
+        return lambda v, _: jnp.where(sub > 0, pltpu.roll(v, 1, 0), 0.0)
+
+    for step in range(ITERS):
+        step_strips(
+            step, from_block if step == 0 else from_strip, T,
+            lambda side, x: from_block(side, 6, x), closed_ahead, closed_behind,
+        )
+        for x in range(step, WIDE - 1 - step):
+            row = pl.ds(x + 4, 1)
+            SB[6 + step, 0, row] = T[1, 3, x, pl.ds(7, 1), :]
+            SB[6 + step, 1, row] = T[1, 5, x, pl.ds(7, 1), :]
+        post(6 + step)
+        if step < ITERS - 1:
+            for x in range(step + 1, WIDE - 1 - step):
+                row = pl.ds(x + 4, 1)
+                SB[3 + step, 0, row] = T[0, 0, x, pl.ds(0, 1), :]
+                SB[3 + step, 1, row] = T[0, 2, x, pl.ds(0, 1), :]
+            post(3 + step)
+
+    border_arrives((2,))
+    each_border((0, 1, 2), lambda copy, _: copy.wait_send())
+    loads[2].wait()
+    loads[3].wait()
+
     def next_y(v):
         return jnp.where(iy < NY - 1, pltpu.roll(v, NY - 1, 0), 0.0)
 
@@ -184,62 +251,73 @@
     def last_z(v):
         return jnp.where(iz > 0, pltpu.roll(v, 1, 1), 0.0)
 
-    def magnetic(x, step):
+    def magnetic(x):
         s = half(x)
         ex, ey, ez = F[0, x], F[1, x], F[2, x]
-        hx = F[3, x] - s * ((next_y(ez) - ez) - (next_z(ey) - ey))
-        hy = F[4, x] - s * ((next_z(ex) - ex) - (F[2, x + 1] - ez))
-        hz = F[5, x] - s * ((F[1, x + 1] - ey) - (next_y(ex) - ex))
-        F[3, x], F[4, x], F[5, x] = hx, hy, hz
-        row = pl.ds(x + 4, 1)
-        SB[6 + step, 0, row] = hx[NY - 1 : NY]
-        SB[6 + step, 1, row] = hz[NY - 1 : NY]
-        return ex, ey, ez, hx, hy, hz
-
-    def both(x, step, graded):
-        ex, ey, ez, hx, hy, hz = magnetic(x, step)
+        return (
+            F[3, x] - s * ((next_y(ez) - ez) - (next_z(ey) - ey)),
+            F[4, x] - s * ((next_z(ex) - ex) - (F[2, x + 1] - ez)),
+            F[5, x] - s * ((F[1, x + 1] - ey) - (next_y(ex) - ex)),
+        )
+
+    def electric(x):
+        hx, hy, hz = F[3, x], F[4, x], F[5, x]
         c = F[6, x]
-        ex = ex + c * ((hz - last_y(hz)) - (hy - last_z(hy)))
-        ey = ey + c * ((hx - last_z(hx)) - (hz - F[5, x - 1]))
-        ez = ez + c * ((hy - F[4, x - 1]) - (hx - last_y(hx)))
-        F[0, x], F[1, x], F[2, x] = ex, ey, ez
-        if step < ITERS - 1:
-            row = pl.ds(x + 4, 1)
-            SB[3 + step, 0, row] = ex[0:1]
-            SB[3 + step, 1, row] = ez[0:1]
-        if graded:
-            r = x - EDGE
-            g = FE[step, 0, r].astype(F32) * ex + FE[step, 1, r].astype(F32) * ey + FE[step, 2, r].astype(F32) * ez
-            G[r] = g if step == 0 else G[r] + g
-
-    for step in range(ITERS):
-        magnetic(step, step)
-        lax.fori_loop(step + 1, EDGE, lambda x, _: (both(x, step, False), 0)[1], 0)
-        lax.fori_loop(EDGE, EDGE + ROWS, lambda x, _: (both(x, step, True), 0)[1], 0)
-        lax.fori_loop(EDGE + ROWS, WIDE - 1 - step, lambda x, _: (both(x, step, False), 0)[1], 0)
-        post(6 + step)
-        if step < ITERS - 1:
-            post(3 + step)
+        return (
+            F[0, x] + c * ((hz - last_y(hz)) - (hy - last_z(hy))),
+            F[1, x] + c * ((hx - last_z(hx)) - (hz - F[5, x - 1])),
+            F[2, x] + c * ((hy - F[4, x - 1]) - (hx - last_y(hx))),
+        )
+
+    def rows_of(first, trips, group, compute, base):
+        @pl.loop(0, trips)
+        def _(i):
+            rows = [first + group * i + j for j in range(group)]
+            values = [compute(x) for x in rows]
+            for x, value in zip(rows, values):
+                for k in range(3):
+                    F[base + k, x] = value[k]
+
+    G[...] = jnp.zeros(G.shape, F32)
+
+    @pl.loop(0, ITERS)
+    def _(t):
+        rows_of(0, 5, 3, magnetic, 3)
+        rows_of(1, 7, 2, electric, 0)
+
+        @pl.loop(0, ROWS // 2)
+        def _(i):
+            for r in (2 * i, 2 * i + 1):
+                x = r + EDGE
+                G[r] = G[r] + (
+                    FE[t, 0, r].astype(F32) * F[0, x] + FE[t, 1, r].astype(F32) * F[1, x]
+                    + FE[t, 2, r].astype(F32) * F[2, x]
+                )
+
+    for k in range(6):
+        for side in range(2):
+            D[side, k] = jnp.zeros((WIDE, 8, NZ), F32)
 
     lower = sub < 4
 
-    def gather(W, z_send, z_recv, p_send, p_recv):
+    def gather(W, direct, z_send, z_recv, p_send, p_recv):
         def slot(s):
             return W.at[pl.ds(ROWS * s, ROWS)]
 
         def relay(way, k):
             sign = -1 if way == 0 else 1
             return pltpu.make_async_remote_copy(
-                src_ref=slot(8 + sign * 2 * (k - 1)), dst_ref=slot(8 + sign * 2 * k),
+                src_ref=slot(8 if direct else 8 + sign * 2 * (k - 1)), dst_ref=slot(8 + sign * 2 * k),
                 send_sem=z_send.at[way, k - 1], recv_sem=z_recv.at[way, k - 1],
-                device_id={"gx": gx - 2 * sign}, device_id_type=MESH,
+                device_id={"gx": gx - 2 * sign * (k if direct else 1)}, device_id_type=MESH,
             )
 
-        def exists(way, k):
-            return chip >= k if way == 0 else chip + k <= chips - 1
+        exists = chip_at
 
         def relays(way, k):
-            onward = up_chip if way == 0 else down_chip
+            if direct:
+                return chip_at(1 - way, k)
+            onward = chip_at(1 - way, 1)
             return onward if k == 1 else onward & exists(way, k - 1)
 
         def across(way, k):
@@ -261,14 +339,15 @@
             return known
 
         def begin():
-            pl.when(relays(0, 1))(lambda: relay(0, 1).start())
-            pl.when(relays(1, 1))(lambda: relay(1, 1).start())
+            for k in range(CHIPS if direct else 1, 0, -1):
+                for way in (0, 1):
+                    pl.when(relays(way, k))(functools.partial(lambda w, j: relay(w, j).start(), way, k))
             across(0, 0).start()
 
         def step(k):
             for way in (0, 1):
                 pl.when(exists(way, k))(functools.partial(lambda w: relay(w, k).wait_recv(), way))
-                if k < CHIPS:
+                if k < CHIPS and not direct:
                     pl.when(relays(way, k + 1))(functools.partial(lambda w: relay(w, k + 1).start(), way))
                 pl.when(crosses(way, k))(functools.partial(lambda w: across(w, k).start(), way))
 
@@ -291,8 +370,8 @@
 
         return begin, step, finish, drain
 
-    begin_a, step_a, finish_a, drain_a = gather(WA, za_send, za_recv, pa_send, pa_recv)
-    begin_b, step_b, finish_b, drain_b = gather(WB, zb_send, zb_recv, pb_send, pb_recv)
+    begin_a, step_a, finish_a, drain_a = gather(WA, False, za_send, za_recv, pa_send, pa_recv)
+    begin_b, step_b, finish_b, drain_b = gather(WB, False, zb_send, zb_recv, pb_send, pb_recv)
 
     @pl.loop(0, ROWS)
     def _(r):
@@ -300,9 +379,6 @@
         WA[8 * ROWS + r, pl.ds(0, 16), :] = m[8:24]
         WA[8 * ROWS + r, pl.ds(16, 8), :] = jnp.where(lower, m[24:32], m[0:8])
 
-    begin_a()
-    for k in range(1, CHIPS + 1):
-        step_a(k)
 
     def forward(m, way):
         tile = 2 if way == 0 else 0
@@ -312,15 +388,12 @@
             send_sem=fwd_send.at[m, way], recv_sem=fwd_recv.at[m, way], device_id=where, device_id_type=MESH,
         )
 
+    begin_a()
     order = (0, 1, 2, 6, 3, 7, 4, 8, 5, 9)
     for m in order:
         pl.when(receives(m))(functools.partial(lambda i: far(i).wait_recv(), m))
         pl.when(receives(m) & has_left)(functools.partial(lambda i: forward(i, 0).start(), m))
         pl.when(receives(m) & has_right)(functools.partial(lambda i: forward(i, 1).start(), m))
-
-    for k in range(6):
-        for side in range(2):
-            D[side, k] = jnp.zeros((WIDE, 8, NZ), F32)
 
     def arrived(m):
         pl.when(receives(m) & has_right)(functools.partial(lambda i: forward(i, 0).wait_recv(), m))
@@ -340,62 +413,39 @@
 
     inflow = jnp.where(has_below, 1.0, 0.0).astype(F32)
 
-    def next_s(v, trace):
-        return pltpu.roll(v, 7, 0) + jnp.where(sub == 7, trace, 0.0)
-
-    def last_s(v, trace):
-        return pltpu.roll(v, 1, 0) + jnp.where(sub == 0, trace, 0.0)
-
-    def up(v):
-        return jnp.where(lane < NZ - 1, pltpu.roll(v, NZ - 1, 1), 0.0)
-
-    def down(v):
-        return jnp.where(lane > 0, pltpu.roll(v, 1, 1), 0.0)
-
-    def strip_magnetic(side, x, step):
-        s = half(x)
-        row = pl.ds(x + 4, 1)
-        if side == 0:
-            tx, tz = SB[2 + step, 0, row] * inflow, SB[2 + step, 1, row] * inflow
-        else:
-            tx, tz = RB[2 + step, 0, row], RB[2 + step, 1, row]
-        ex, ey, ez = D[side, 0, x], D[side, 1, x], D[side, 2, x]
-        hx = D[side, 3, x] - s * ((next_s(ez, tz) - ez) - (up(ey) - ey))
-        hy = D[side, 4, x] - s * ((up(ex) - ex) - (D[side, 2, x + 1] - ez))
-        hz = D[side, 5, x] - s * ((D[side, 1, x + 1] - ey) - (next_s(ex, tx) - ex))
-        D[side, 3, x], D[side, 4, x], D[side, 5, x] = hx, hy, hz
-        return ex, ey, ez, hx, hy, hz
-
-    def strip_both(side, x, step, graded):
-        ex, ey, ez, hx, hy, hz = strip_magnetic(side, x, step)
-        row = pl.ds(x + 4, 1)
-        planes = RB if side == 0 else SB
-        tx, tz = planes[6 + step, 0, row], planes[6 + step, 1, row]
-        c = CS[side, x]
-        ex = ex + c * ((hz - last_s(hz, tz)) - (hy - down(hy)))
-        ey = ey + c * ((hx - down(hx)) - (hz - D[side, 5, x - 1]))
-        ez = ez + c * ((hy - D[side, 4, x - 1]) - (hx - last_s(hx, tx)))
-        D[side, 0, x], D[side, 1, x], D[side, 2, x] = ex, ey, ez
-        if graded:
-            r = x - EDGE
-            if side == 0:
-                stored = [FE[step, k, r, pl.ds(0, 16), :].astype(F32)[0:8] for k in range(3)]
-            else:
-                stored = [FE[step, k, r, pl.ds(16, 16), :].astype(F32)[8:16] for k in range(3)]
-            g = stored[0] * ex + stored[1] * ey + stored[2] * ez
-            GS[side, r] = g if step == 0 else GS[side, r] + g
-
-    def strips(x, step, graded):
-        strip_both(0, x, step, graded)
-        strip_both(1, x, step, graded)
-        return 0
-
+    def strip(side, k, x):
+        return D[side, k, x]
+
+    def open_ahead(step):
+        def ahead_at(side, x):
+            planes, row = (SB if side == 0 else RB), pl.ds(x + 4, 1)
+
+            def ahead(v, comp):
+                trace = planes[2 + step, comp, row]
+                trace = trace * inflow if side == 0 else trace
+                return pltpu.roll(v, 7, 0) + jnp.where(sub == 7, trace, 0.0)
+
+            return ahead
+
+        return ahead_at
+
+    def open_behind(step):
+        def behind_at(side, x):
+            planes, row = (RB if side == 0 else SB), pl.ds(x + 4, 1)
+            return lambda v, comp: pltpu.roll(v, 1, 0) + jnp.where(sub == 0, planes[6 + step, comp, row], 0.0)
+
+        return behind_at
+
+    half_tile = (pl.ds(0, 16), pl.ds(NY - 16, 16))
     for step in range(ITERS):
-        strip_magnetic(0, step, step)
-        strip_magnetic(1, step, step)
-        lax.fori_loop(step + 1, EDGE, lambda x, _: strips(x, step, False), 0)
-        lax.fori_loop(EDGE, EDGE + ROWS, lambda x, _: strips(x, step, True), 0)
-        lax.fori_loop(EDGE + ROWS, WIDE - 1 - step, lambda x, _: strips(x, step, False), 0)
+        step_strips(step, strip, D, lambda side, x: CS[side, x], open_ahead(step), open_behind(step))
+        for r in range(ROWS):
+            for side in range(2):
+                stored = [FE[step, k, r, half_tile[side], :].astype(F32) for k in range(3)]
+                stored = [v[0:8] if side == 0 else v[8:16] for v in stored]
+                e = [D[side, k, r + EDGE] for k in range(3)]
+                g = stored[0] * e[0] + stored[1] * e[1] + stored[2] * e[2]
+                GS[side, r] = g if step == 0 else GS[side, r] + g
 
     @pl.loop(0, ROWS)
     def _(r):
@@ -403,6 +453,7 @@
         mask = jnp.where(lower, MV[r, pl.ds(0, 8), :], MV[r, pl.ds(24, 8), :])
         WB[8 * ROWS + r] = g * mask.astype(F32)
 
+    step_a(1)
     begin_b()
 
     @pl.loop(0, ROWS)
@@ -414,9 +465,11 @@
             final_ref[k, r, pl.ds(0, 8), :] = e[0:8] + jnp.where(lower, D[0, k, x], 0.0)
             final_ref[k, r, pl.ds(24, 8), :] = e[24:32] + jnp.where(lower, 0.0, D[1, k, x])
 
+    for k in range(1, CHIPS + 1):
+        if k > 1:
+            step_a(k)
+        step_b(k)
     finish_a()
-    for k in range(1, CHIPS + 1):
-        step_b(k)
     finish_b()
 
     taps = [tap_ref[b] for b in range(BAND)]
@@ -446,7 +499,7 @@
 
     def shards(adjoint_fields, forward_e, permittivity, design_mask, band_offsets, filter_taps):
         dma = pltpu.SemaphoreType.DMA
-        hbm, vmem, smem = (pl.BlockSpec(memory_space=s) for s in (pl.ANY, pltpu.VMEM, pltpu.SMEM))
+        hbm, vmem, smem = (pl.BlockSpec(memory_space=s) for s in (pltpu.HBM, pltpu.VMEM, pltpu.SMEM))
         return pl.pallas_call(
             functools.partial(kernel, nx, ny),
             out_shape=(
@@ -464,18 +517,22 @@
                 pltpu.VMEM((MESSAGES, 2, 24, NZ), F32),
                 pltpu.VMEM((MESSAGES, 2, 24, NZ), F32),
                 pltpu.VMEM((2, 6, WIDE, 8, NZ), F32),
+                pltpu.VMEM((2, 6, WIDE, 8, NZ), F32),
                 pltpu.VMEM((2, WIDE, 8, NZ), F32),
                 pltpu.VMEM((2, ROWS, 8, NZ), F32),
                 pltpu.VMEM((17 * ROWS, 24, NZ), F32),
                 pltpu.VMEM((17 * ROWS, 8, NZ), F32),
-                dma((4,)), dma((2,)), dma((2,)),
+                dma((4,)), dma((2, 3)), dma((2, 3)),
                 dma((MESSAGES,)), dma((MESSAGES,)), dma((MESSAGES, 2)), dma((MESSAGES, 2)),
                 dma((2, CHIPS)), dma((2, CHIPS)), dma((9,)), dma((8,)),
                 dma((2, CHIPS)), dma((2, CHIPS)), dma((9,)), dma((8,)),
             ],
-            compiler_params=pltpu.CompilerParams(collective_id=0, has_side_effects=True),
+            compiler_params=pltpu.CompilerParams(collective_id=0, has_side_effects=True, vmem_limit_bytes=16 << 20),
             name="adjoint_yee_filter",
-        )(adjoint_fields, forward_e, permittivity, design_mask, band_offsets, filter_taps)
+        )(
+            *(pltpu.with_memory_space_constraint(a, pltpu.HBM) for a in (adjoint_fields, forward_e, permittivity, design_mask)),
+            band_offsets, filter_taps,
+        )
 
     return jax.shard_map(
         shards,

time: 101 us -> 79.8 us (0.79)
  Pallas kernels: 96.1 us -> 76.3 us
    pallas_call x1, Pallas kernels: 96.1 us -> 76.3 us  [shards(): pl.pallas_call(functools.partial(kernel, nx, ny), out_shape=(jax.ShapeDty...]
    unnamed x2 -> x6, local copies, waits for them, and re-layouts: 3.33 us -> 2.71 us
where the time goes in v2:
time: 79.8 us; the launch traced here: 79.7 us
  Pallas kernels  76.3 us (96%)
  local copies, waits for them, and re-layouts  2.71 us (3%)
    pallas_call x1, Pallas kernels, shards(): pl.pallas_call(functools.partial(kernel, nx, ny), out_shape=(jax.ShapeDty...  76.3 us
    unnamed x6, local copies, waits for them, and re-layouts  2.71 us

profile of v2, /device:TPU:7, one launch (start us, length us, event | category | flops | bytes accessed | tf_op | source)
XLA Modules:
  0.0 79.7 jit_solution(1890411607792822444)
XLA Ops:
  0.6 0.0 copy-start
  0.6 0.6 copy-done
  1.3 0.0 copy-start.1
  1.3 0.7 copy-done.1
  1.9 76.3 %adjoint_yee_filter.1 = (f32[8,32,128]{2,1,0:T(8,128)S(1)}, f32[3,8,32,128]{3,2,1,0:T(8,128)S(1)}) custom-call(f32[6,8,32,128]{3,2,1,0:T(8,128)} %fields_hbm.1, bf16[4,3,8,32,128]{4,3,2,1,0:T(8,128)(2,1)} %stored_hbm.1, f32[8,32,128]{2,1,0:T(8,128)} %perm_hbm.1, s32[8,32,128]{2,1,0:T(8,128)} %mask_hbm.1, s32[9]{0:T(128)S(1)} %copy-done, f32[9]{0:T(128)S(1)} %copy-done.1), custom_call_target="tpu_custom_call" | custom-call | tf_op jit(solution)/shard_map/adjoint_yee_filter/pallas_call | solution.py:503
  78.3 0.7 copy.10
  78.9 0.7 copy.11
Async XLA Ops:
  0.6 0.7 copy-start
  1.3 0.7 copy-start.1

commit v3 on v2

--- a/solution.py
+++ b/solution.py
@@ -27,9 +27,9 @@
 
 def kernel(
     nx, ny,
-    fields_hbm, stored_hbm, perm_hbm, mask_hbm, off_ref, tap_ref,
+    fields_hbm, stored_hbm, perm_hbm, mask_hbm, off_hbm, tap_hbm,
     filt_ref, final_ref,
-    F, FE, PV, MV, G, SB, RB, T, D, CS, GS, WA, WB,
+    F, FE, PV, MV, G, SB, RB, T, D, CS, GS, WA, WB, off_ref, tap_ref,
     load_sem, x_send, x_recv, far_send, far_recv, fwd_send, fwd_recv,
     za_send, za_recv, pa_send, pa_recv, zb_send, zb_recv, pb_send, pb_recv,
 ):
@@ -43,6 +43,8 @@
         pltpu.make_async_copy(perm_hbm, PV, load_sem.at[1]),
         pltpu.make_async_copy(stored_hbm, FE, load_sem.at[2]),
         pltpu.make_async_copy(mask_hbm, MV, load_sem.at[3]),
+        pltpu.make_async_copy(off_hbm, off_ref, load_sem.at[4]),
+        pltpu.make_async_copy(tap_hbm, tap_ref, load_sem.at[5]),
     ]
     for load in loads:
         load.start()
@@ -237,7 +239,8 @@
     border_arrives((2,))
     each_border((0, 1, 2), lambda copy, _: copy.wait_send())
     loads[2].wait()
-    loads[3].wait()
+    for load in loads[3:]:
+        load.wait()
 
     def next_y(v):
         return jnp.where(iy < NY - 1, pltpu.roll(v, NY - 1, 0), 0.0)
@@ -497,16 +500,16 @@
 def solution(mesh):
     nx, ny = mesh.shape["gx"], mesh.shape["gy"]
 
-    def shards(adjoint_fields, forward_e, permittivity, design_mask, band_offsets, filter_taps):
+    def shards(*arguments):
         dma = pltpu.SemaphoreType.DMA
-        hbm, vmem, smem = (pl.BlockSpec(memory_space=s) for s in (pltpu.HBM, pltpu.VMEM, pltpu.SMEM))
+        hbm, vmem = (pl.BlockSpec(memory_space=s) for s in (pltpu.HBM, pltpu.VMEM))
         return pl.pallas_call(
             functools.partial(kernel, nx, ny),
             out_shape=(
                 jax.ShapeDtypeStruct((ROWS, NY, NZ), F32),
                 jax.ShapeDtypeStruct((3, ROWS, NY, NZ), F32),
             ),
-            in_specs=[hbm, hbm, hbm, hbm, smem, smem],
+            in_specs=[hbm] * 6,
             out_specs=(vmem, vmem),
             scratch_shapes=[
                 pltpu.VMEM((7, WIDE, NY, NZ), F32),
@@ -522,7 +525,8 @@
                 pltpu.VMEM((2, ROWS, 8, NZ), F32),
                 pltpu.VMEM((17 * ROWS, 24, NZ), F32),
                 pltpu.VMEM((17 * ROWS, 8, NZ), F32),
-                dma((4,)), dma((2, 3)), dma((2, 3)),
+                pltpu.SMEM((BAND,), jnp.int32), pltpu.SMEM((BAND,), F32),
+                dma((6,)), dma((2, 3)), dma((2, 3)),
                 dma((MESSAGES,)), dma((MESSAGES,)), dma((MESSAGES, 2)), dma((MESSAGES, 2)),
                 dma((2, CHIPS)), dma((2, CHIPS)), dma((9,)), dma((8,)),
                 dma((2, CHIPS)), dma((2, CHIPS)), dma((9,)), dma((8,)),
@@ -530,8 +534,7 @@
             compiler_params=pltpu.CompilerParams(collective_id=0, has_side_effects=True, vmem_limit_bytes=16 << 20),
             name="adjoint_yee_filter",
         )(
-            *(pltpu.with_memory_space_constraint(a, pltpu.HBM) for a in (adjoint_fields, forward_e, permittivity, design_mask)),
-            band_offsets, filter_taps,
+            *(pltpu.with_memory_space_constraint(a, pltpu.HBM) for a in arguments),
         )
 
     return jax.shard_map(

time: 79.8 us -> 78 us (0.977)
  local copies, waits for them, and re-layouts: 2.71 us -> 1.4 us
    unnamed x6 -> x2, local copies, waits for them, and re-layouts: 2.71 us -> 1.4 us
where the time goes in v3:
time: 78 us; the launch traced here: 77.9 us
  Pallas kernels  75.8 us (97%)
  local copies, waits for them, and re-layouts  1.4 us (2%)
    pallas_call x1, Pallas kernels, shards(): pl.pallas_call(functools.partial(kernel, nx, ny), out_shape=(jax.ShapeDty...  75.8 us

profile of v3, /device:TPU:7, one launch (start us, length us, event | category | flops | bytes accessed | tf_op | source)
XLA Modules:
  0.0 77.9 jit_solution(1030552157894626461)
XLA Ops:
  0.6 75.8 %adjoint_yee_filter.1 = (f32[8,32,128]{2,1,0:T(8,128)S(1)}, f32[3,8,32,128]{3,2,1,0:T(8,128)S(1)}) custom-call(f32[6,8,32,128]{3,2,1,0:T(8,128)} %fields_hbm.1, bf16[4,3,8,32,128]{4,3,2,1,0:T(8,128)(2,1)} %stored_hbm.1, f32[8,32,128]{2,1,0:T(8,128)} %perm_hbm.1, s32[8,32,128]{2,1,0:T(8,128)} %mask_hbm.1, s32[9]{0:T(128)} %off_hbm.1, f32[9]{0:T(128)} %tap_hbm.1), custom_call_target="tpu_custom_call" | custom-call | tf_op jit(solution)/shard_map/adjoint_yee_filter/pallas_call | solution.py:506
  76.5 0.7 copy.10
  77.1 0.7 copy.11

commit v4 on v3

--- a/solution.py
+++ b/solution.py
@@ -88,9 +88,8 @@
     greet(has_above, {"gy": gy + 1})
     greet(has_left, {"gx": gx - 1})
     greet(has_right, {"gx": gx + 1})
-    for k in range(1, CHIPS + 1):
-        greet(chip_at(0, k), {"gx": gx - 2 * k})
-        greet(chip_at(1, k), {"gx": gx + 2 * k})
+    greet(down_chip, {"gx": gx - 2})
+    greet(up_chip, {"gx": gx + 2})
 
     iy = lax.broadcasted_iota(jnp.int32, (NY, NZ), 0)
     iz = lax.broadcasted_iota(jnp.int32, (NY, NZ), 1)
@@ -125,7 +124,7 @@
     pl.semaphore_wait(
         barrier,
         count(has_below) + count(has_above) + count(has_left) + count(has_right)
-        + jnp.minimum(chip, CHIPS) + jnp.minimum(chips - 1 - chip, CHIPS),
+        + count(down_chip) + count(up_chip),
     )
 
     pieces = (pl.ds(0, 8), pl.ds(NY - 8, 8), pl.ds(8, NY - 16))

time: 78 us -> 77.4 us (level)
  no operation moved by 1% of the time
where the time goes in v4:
time: 77.4 us; the launch traced here: 77.1 us
  Pallas kernels  75.1 us (97%)
  local copies, waits for them, and re-layouts  1.4 us (2%)
    pallas_call x1, Pallas kernels, shards(): pl.pallas_call(functools.partial(kernel, nx, ny), out_shape=(jax.ShapeDty...  75.1 us

profile of v4, /device:TPU:7, one launch (start us, length us, event | category | flops | bytes accessed | tf_op | source)
XLA Modules:
  0.0 77.1 jit_solution(17067413057720477990)
XLA Ops:
  0.6 75.1 %adjoint_yee_filter.1 = (f32[8,32,128]{2,1,0:T(8,128)S(1)}, f32[3,8,32,128]{3,2,1,0:T(8,128)S(1)}) custom-call(f32[6,8,32,128]{3,2,1,0:T(8,128)} %fields_hbm.1, bf16[4,3,8,32,128]{4,3,2,1,0:T(8,128)(2,1)} %stored_hbm.1, f32[8,32,128]{2,1,0:T(8,128)} %perm_hbm.1, s32[8,32,128]{2,1,0:T(8,128)} %mask_hbm.1, s32[9]{0:T(128)} %off_hbm.1, f32[9]{0:T(128)} %tap_hbm.1), custom_call_target="tpu_custom_call" | custom-call | tf_op jit(solution)/shard_map/adjoint_yee_filter/pallas_call | solution.py:505
  75.7 0.7 copy.10
  76.4 0.7 copy.11
